TPU v7x, 32 devices: a whole 2x2x4 slice. The times are simulated.
32 devices in a mesh: seq: 8 (over y, x, core), exp: 4 (over z).
Axes of the slice: x: 2, y: 2, z: 4, core: 2. Of those that a mesh axis runs over, the one named last changes fastest.
Arguments:
- queries: bfloat16 [1024, 2048], P('seq', 'exp'), may hold values from -10 to 10
- key_rows: bfloat16 [1024, 2048], P('seq', 'exp'), may hold values from -10 to 10
- value_rows: bfloat16 [1024, 2048], P('seq', 'exp'), may hold values from -6 to 6
- residual: bfloat16 [1024, 2048], P('seq'), may hold values from -20 to 20
- out_weight: bfloat16 [2048, 2048], P('exp'), may hold values from -1 to 1
- norm_gain: float32 [2048], replicated, may hold values from 0.5 to 1.5
- gate_weight: bfloat16 [16, 2048, 1408], P('seq', None, 'exp'), may hold values from -0.125 to 0.125
- up_weight: bfloat16 [16, 2048, 1408], P('seq', None, 'exp'), may hold values from -0.125 to 0.125
- down_weight: bfloat16 [16, 1408, 2048], P('seq', 'exp'), may hold values from -0.15625 to 0.15625
- routes: int32 [1024, 6], P('seq'), may hold values from 0 to 15, all different within a row; in each aligned block of 128 rows (0 to 127, 128 to 255, ...) at most 96 rows name the same one
- route_gates: float32 [1024, 6], P('seq'), may hold values from 0.2 to 1
- block_picks: int32 [2, 3], replicated, may hold values from 0 to 1, as said below
Outputs:
- layer_out: bfloat16 [1024, 2048], P(('seq', 'exp'))
Inputs may be any that keep to these rules, and one draw needn't show every extreme that they name: `block_picks`: row b names block b first, then blocks at or before b, repeats allowed. `routes`: in each aligned block of 128 rows no expert is named by more than 96 rows, a bound that some block reaches.
All inputs are finite; a program needn't handle non-finite values.
Results may differ from a plain program's by a relative error of at most 0.015.
Values may be sent and summed in bfloat16 or wider, within the bound.
No kernel may reach another device: no remote copies, remote signals or barrier semaphores. Data moves between devices by JAX's collectives and lax.ppermute only.
A program may use at most 64 MiB of HBM per device.

v0:
```python
import jax
import jax.numpy as jnp
from jax import lax
from jax.sharding import PartitionSpec as P

HD = 128
TOPK = 6
BLK = 512


def rms_scale(hidden, norm_gain):
    mean_square = jnp.mean(hidden * hidden, axis=-1, keepdims=True)
    return hidden * lax.rsqrt(mean_square + 1e-06) * norm_gain


def expert_block(arrived, gate_weight, up_weight, down_weight):
    gate_part = jnp.einsum(
        "semd,edf->semf", arrived, gate_weight, preferred_element_type=jnp.float32
    )
    up_part = jnp.einsum("semd,edf->semf", arrived, up_weight, preferred_element_type=jnp.float32)
    inner_act = (jax.nn.silu(gate_part) * up_part).astype(jnp.bfloat16)
    return jnp.einsum(
        "semf,efd->semd", inner_act, down_weight, preferred_element_type=jnp.float32
    ).astype(jnp.bfloat16)


def per_device(
    queries,
    key_rows,
    value_rows,
    residual,
    out_weight,
    norm_gain,
    gate_weight,
    up_weight,
    down_weight,
    routes,
    route_gates,
    block_picks,
):
    seq_count = lax.axis_size("seq")
    exp_count = lax.axis_size("exp")
    seq_index = lax.axis_index("seq")
    exp_index = lax.axis_index("exp")
    tok_rows = queries.shape[0]
    head_count = queries.shape[1] // HD
    nblocks = block_picks.shape[0]
    model_width = residual.shape[1]
    positions = seq_index * tok_rows + jnp.arange(tok_rows, dtype=jnp.int32)
    block_ids = jnp.arange(nblocks, dtype=jnp.int32)
    chosen = jnp.any(block_picks[:, :, None] == block_ids[None, None, :], axis=1).astype(
        jnp.float32
    )
    query_onehot = ((positions // BLK)[:, None] == block_ids[None, :]).astype(jnp.float32)
    query_allowed = jnp.dot(query_onehot, chosen)
    split_queries = queries.reshape(tok_rows, head_count, HD)
    score_scale = HD ** (-0.5)
    run_max = jnp.full((tok_rows, head_count), -1e30, jnp.float32)
    key_piece = lax.all_gather(key_rows, "seq", axis=0, tiled=True)
    value_piece = lax.all_gather(value_rows, "seq", axis=0, tiled=True)
    piece_rows = key_piece.shape[0]
    key_pos = jnp.arange(piece_rows, dtype=jnp.int32)
    key_onehot = ((key_pos // BLK)[:, None] == block_ids[None, :]).astype(jnp.float32)
    allowed = (
        (jnp.dot(query_allowed, key_onehot.T) > 0.5) & (key_pos[None, :] <= positions[:, None])
    )[:, None, :]
    scores = (
        jnp.einsum(
            "qhd,khd->qhk",
            split_queries,
            key_piece.reshape(piece_rows, head_count, HD),
            preferred_element_type=jnp.float32,
        )
        * score_scale
    )
    piece_max = jnp.max(jnp.where(allowed, scores, -1e30), axis=2)
    new_max = jnp.maximum(run_max, piece_max)
    expo = jnp.where(allowed, jnp.exp(scores - new_max[:, :, None]), 0.0)
    new_total = jnp.sum(expo, axis=2)
    mixed_values = jnp.einsum(
        "qhk,khd->qhd",
        expo.astype(jnp.bfloat16),
        value_piece.reshape(piece_rows, head_count, HD),
        preferred_element_type=jnp.float32,
    )
    attended = (
        (mixed_values / new_total[:, :, None])
        .astype(jnp.bfloat16)
        .reshape(tok_rows, head_count * HD)
    )
    proj_part = jnp.dot(attended, out_weight, preferred_element_type=jnp.float32)
    share_rows = tok_rows // exp_count
    projected = lax.psum_scatter(
        proj_part.astype(jnp.bfloat16), "exp", scatter_dimension=0, tiled=True
    ).astype(jnp.float32)
    own_residual = lax.dynamic_slice_in_dim(residual, exp_index * share_rows, share_rows, 0).astype(
        jnp.float32
    )
    own_hidden = own_residual + projected
    own_normed = rms_scale(own_hidden, norm_gain).astype(jnp.bfloat16)
    normed = lax.all_gather(own_normed, "exp", axis=0, tiled=True)
    local_experts = gate_weight.shape[0]
    expert_count = local_experts * seq_count
    slot_most = exp_count * max(1, 2 * tok_rows * TOPK // (expert_count * exp_count))
    slot_total = expert_count * slot_most
    pair_count = tok_rows * TOPK
    flat_routes = routes.reshape(pair_count)
    route_onehot = (
        flat_routes[:, None] == jnp.arange(expert_count, dtype=jnp.int32)[None, :]
    ).astype(jnp.int32)
    slot_rank = jnp.sum((jnp.cumsum(route_onehot, axis=0) - 1) * route_onehot, axis=1)
    slot_ids = flat_routes * slot_most + slot_rank
    sources = (
        jnp.full((slot_total,), pair_count, jnp.int32)
        .at[slot_ids]
        .set(jnp.arange(pair_count, dtype=jnp.int32))
    )
    live_slot = sources < pair_count
    token_ids = jnp.minimum(sources, pair_count - 1) // TOPK
    outgoing = jnp.where(live_slot[:, None], normed[token_ids], jnp.zeros((), jnp.bfloat16))
    outgoing = outgoing.reshape(seq_count, local_experts, slot_most, model_width)
    returned = lax.all_to_all(
        expert_block(
            lax.all_to_all(outgoing, "seq", split_axis=0, concat_axis=0, tiled=True),
            gate_weight,
            up_weight,
            down_weight,
        ),
        "seq",
        split_axis=0,
        concat_axis=0,
        tiled=True,
    )
    back_rows = returned.reshape(slot_total, model_width)[slot_ids].astype(jnp.float32)
    weighted = back_rows.reshape(tok_rows, TOPK, model_width) * route_gates[:, :, None]
    mixture_part = jnp.sum(weighted, axis=1)
    own_mixture = lax.psum_scatter(
        mixture_part.astype(jnp.bfloat16), "exp", scatter_dimension=0, tiled=True
    ).astype(jnp.float32)
    return (own_hidden + own_mixture).astype(jnp.bfloat16)


def solution(mesh):
    placed = (
        P("seq", "exp"),
        P("seq", "exp"),
        P("seq", "exp"),
        P("seq", None),
        P("exp", None),
        P(),
        P("seq", None, "exp"),
        P("seq", None, "exp"),
        P("seq", "exp", None),
        P("seq", None),
        P("seq", None),
        P(),
    )
    return jax.shard_map(
        per_device, mesh=mesh, in_specs=placed, out_specs=P(("seq", "exp"), None), check_vma=False
    )
```

profile of v0, /device:TPU:0, one launch (start us, length us, event | category | flops | bytes accessed | tf_op | source)
XLA Modules:
  0.0 345.7 jit_solution(12460206369254408509)
XLA Ops:
  6.5 0.0 copy-start
  6.5 0.0 all-gather.3.cloned.1.call-start
  6.5 1.8 copy.47
  8.4 0.0 all-gather.3.cloned.1.call-update
  8.4 0.0 all-gather.5.cloned.1.call-start
  8.4 0.7 all-gather.5.cloned.1.call-update
  9.1 0.0 reduce-scatter.3.cloned.1.call-start
  9.2 0.8 fusion.49
  10.0 0.6 fusion.27
  10.5 0.3 copy.46
  10.8 0.8 copy.53
  11.6 0.1 eq.77
  11.8 1.7 reduce-window.6
  13.5 22.0 %all-gather.3.cloned.1.call-done = bf16[1024,512]{0,1:T(8,128)(2,1)} async-done(((bf16[128,512]{0,1:T(8,128)(2,1)}), bf16[1024,512]{0,1:T(8,128)(2,1)}) %all-gather.3.cloned.1.call-update) | async-done | bytes 1048592 | tf_op jit(solution)/shard_map/all_gather | solution.py:59
  35.4 1.9 fusion.11
  37.3 0.0 copy-start.2
  37.3 1.3 copy-done.2
  38.7 0.5 fusion.22
  39.1 21.6 %all-gather.5.cloned.1.call-done = bf16[1024,512]{1,0:T(8,128)(2,1)} async-done(((bf16[128,512]{1,0:T(8,128)(2,1)}), bf16[1024,512]{1,0:T(8,128)(2,1)}) %all-gather.5.cloned.1.call-update) | async-done | bytes 1048592 | tf_op jit(solution)/shard_map/all_gather | solution.py:60
  60.7 2.3 copy.50
  63.0 0.0 copy-start.4
  63.0 2.7 fusion.26
  65.8 0.0 copy-start.6
  65.8 0.0 copy-start.7
  65.8 0.0 copy-done.4
  65.8 1.3 convolution_convert_fusion
  67.1 0.0 reduce-scatter.3.cloned.1.call-update
  67.1 0.2 slice_reduce_fusion
  67.3 0.1 eq.73
  67.5 0.0 copy-done.6
  67.5 0.1 copy.52
  67.6 0.1 mul.75
  67.8 0.1 fusion.40
  67.9 3.4 scatter_custom_fusion
  71.3 0.1 broadcast_in_dim.60
  71.4 17.6 %reduce-scatter.3.cloned.1.call-done = bf16[32,2048]{1,0:T(8,128)(2,1)} async-done(((bf16[128,2048]{1,0:T(8,128)(2,1)}), bf16[32,2048]{1,0:T(8,128)(2,1)}) %reduce-scatter.3.cloned.1.call-update) | async-done | bytes 131088 | tf_op jit(solution)/shard_map/reduce_scatter | solution.py:93
  89.1 1.1 multiply_reduce_fusion.1
  90.2 0.0 copy-done.7
  90.2 1.1 multiply_convert_fusion
  91.3 15.4 %all_gather.11 = bf16[128,2048]{1,0:T(8,128)(2,1)S(1)} all-gather(bf16[32,2048]{1,0:T(8,128)(2,1)S(1)} %multiply_convert_fusion), channel_id=1, replica_groups=mesh['seq'=8,'exp'=4] {'exp'}, dimensions={0}, use_global_device_ids=true | all-gather | bytes 655360 | tf_op jit(solution)/shard_map/all_gather | solution.py:101
  106.6 7.1 %gather_fusion = bf16[1536,2048]{1,0:T(8,128)(2,1)} fusion(bf16[128,2048]{1,0:T(8,128)(2,1)S(1)} %all_gather.11, s32[2048]{0:T(1024)S(1)} %pad_clamp_fusion), kind=kCustom, calls=%fused_computation | custom fusion | bytes 12589056 | tf_op jit(solution)/shard_map/gather | solution.py:120
  113.7 3.3 broadcast_select_fusion
  117.0 0.0 copy-start.9
  117.0 75.3 %all_to_all.10 = bf16[8,2,96,2048]{3,2,1,0:T(8,128)(2,1)S(1)} all-to-all(bf16[8,2,96,2048]{3,2,1,0:T(8,128)(2,1)S(1)} %broadcast_select_fusion), channel_id=1, replica_groups=mesh['seq'=8,'exp'=4] {'seq'}, dimensions={0} | all-to-all | bytes 12582912 | tf_op jit(solution)/shard_map/all_to_all | solution.py:124
  192.4 0.0 copy-start.3
  192.4 2.7 copy-done.3
  195.0 0.0 copy-done.9
  195.0 4.8 %fusion.2 = f32[2,8,96,352]{3,2,1,0:T(8,128)} fusion(bf16[8,2,96,2048]{3,2,1,0:T(8,128)(2,1)S(1)} %all_to_all.10, bf16[2,2048,352]{1,2,0:T(8,128)(2,1)S(1)} %copy-done.9), kind=kOutput, calls=%fused_computation.8 | convolution fusion | flops 2214592512 | bytes 11337728 | tf_op jit(solution)/shard_map/semd,edf->semf/dot_general | solution.py:17
  199.9 0.0 copy-done
  199.9 11.2 %convert_bitcast_fusion = bf16[8,2,96,2048]{3,2,0,1:T(8,128)(2,1)} fusion(bf16[2,352,2048]{2,1,0:T(8,128)(2,1)S(1)} %copy-done, f32[2,8,96,352]{3,2,1,0:T(8,128)} %fusion.2, bf16[2,2048,352]{1,2,0:T(8,128)(2,1)} %param.19, bf16[8,2,96,2048]{3,2,1,0:T(8,128)(2,1)} %copy-done.3), kind=kOutput, calls=%fused_computation.4 | convolution fusion | flops 4435574784 | bytes 20512768 | tf_op jit(solution)/shard_map/semf,efd->semd/dot_general | solution.py:22
  211.1 6.6 %copy.58 = bf16[8,2,96,2048]{3,2,1,0:T(8,128)(2,1)} copy(bf16[8,2,96,2048]{3,2,0,1:T(8,128)(2,1)} %convert_bitcast_fusion) | data formatting | bytes 12582912 | tf_op jit(solution)/shard_map/convert_element_type | solution.py:24
  217.7 4.9 %all-to-all-start.1 = ((bf16[8,2,96,2048]{3,2,1,0:T(8,128)(2,1)}), bf16[8,2,96,2048]{3,2,1,0:T(8,128)(2,1)}, u32[]{:S(2)}, u32[]{:S(2)}) async-start(bf16[8,2,96,2048]{3,2,1,0:T(8,128)(2,1)} %copy.58), calls=%async_computation.2 | async-start | bytes 12582912 | tf_op jit(solution)/shard_map/all_to_all | solution.py:122
  222.6 0.3 reduce-scatter.5.cloned.1.call-start
  222.8 0.0 copy-done.8
  222.8 0.1 copy.59
  223.0 71.2 %all-to-all-done.1 = bf16[8,2,96,2048]{3,2,1,0:T(8,128)(2,1)} async-done(((bf16[8,2,96,2048]{3,2,1,0:T(8,128)(2,1)}), bf16[8,2,96,2048]{3,2,1,0:T(8,128)(2,1)}, u32[]{:S(2)}, u32[]{:S(2)}) %all-to-all-start.1) | async-done | bytes 6291488 | tf_op jit(solution)/shard_map/all_to_all | solution.py:122
  294.1 10.7 %gather_fusion.1 = bf16[768,2048]{1,0:T(8,128)(2,1)} fusion(bf16[1536,2048]{1,0:T(8,128)(2,1)} %bitcast.16, s32[1024]{0:T(1024)S(1)} %pad_clamp_fusion.1), kind=kCustom, calls=%fused_computation.1 | custom fusion | bytes 6294528 | tf_op jit(solution)/shard_map/gather | solution.py:134
  304.8 6.7 %reshape.131 = f32[128,6,2048]{2,1,0:T(8,128)} reshape(bf16[768,2048]{1,0:T(8,128)(2,1)} %gather_fusion.1) | data formatting | bytes 9437184 | tf_op jit(solution)/shard_map/convert_element_type | solution.py:134
  311.5 7.4 %multiply_reduce_fusion = bf16[128,2048]{1,0:T(8,128)(2,1)} fusion(f32[128,6,2048]{2,1,0:T(8,128)} %reshape.131, f32[128,6]{1,0:T(8,128)S(1)} %copy.59), kind=kLoop, calls=%fused_computation.3 | loop fusion | flops 2883584 | bytes 6818816 | tf_op jit(solution)/shard_map/reduce_sum | solution.py:136
  319.0 0.0 reduce-scatter.5.cloned.1.call-update
  319.0 18.5 %reduce-scatter.5.cloned.1.call-done = bf16[32,2048]{1,0:T(8,128)(2,1)} async-done(((bf16[128,2048]{1,0:T(8,128)(2,1)}), bf16[32,2048]{1,0:T(8,128)(2,1)}) %reduce-scatter.5.cloned.1.call-update) | async-done | bytes 131088 | tf_op jit(solution)/shard_map/reduce_scatter | solution.py:137
  337.5 0.0 copy-done.5
  337.5 1.7 add_convert_fusion
  339.2 0.0 copy-done.1
  (16 shorter events, 0.1 us)
Async XLA Ops:
  6.5 193.3 %copy-start = (bf16[2,352,2048]{2,1,0:T(8,128)(2,1)S(1)}, bf16[2,352,2048]{2,1,0:T(8,128)(2,1)}, u32[]{:S(2)}) copy-start(bf16[2,352,2048]{2,1,0:T(8,128)(2,1)} %param.20) | copy-start | bytes 8650756
  6.5 28.9 %all-gather.3.cloned.1.call-start = ((), (), s32[]{:S(2)}) async-start(), calls=%async_computation.4 | async-start | bytes 1179648 | tf_op jit(solution)/shard_map/all_gather | solution.py:59
  8.4 52.4 %all-gather.5.cloned.1.call-start = ((), (), s32[]{:S(2)}) async-start(), calls=%async_computation.5 | async-start | bytes 1179648 | tf_op jit(solution)/shard_map/all_gather | solution.py:60
  9.1 79.9 %reduce-scatter.3.cloned.1.call-start = ((), (), s32[]{:S(2)}) async-start(), calls=%async_computation.6 | async-start | bytes 655360 | tf_op jit(solution)/shard_map/reduce_scatter | solution.py:93
  37.3 1.4 copy-start.2
  63.0 2.8 copy-start.4
  65.8 1.7 copy-start.6
  65.8 24.4 %copy-start.7 = (f32[2048]{0:T(1024)S(1)}, f32[2048]{0:T(1024)}, u32[]{:S(2)}) copy-start(f32[2048]{0:T(1024)} %param.17) | copy-start | bytes 24580
  117.0 78.0 %copy-start.9 = (bf16[2,2048,352]{1,2,0:T(8,128)(2,1)S(1)}, bf16[2,2048,352]{1,2,0:T(8,128)(2,1)}, u32[]{:S(2)}) copy-start(bf16[2,2048,352]{1,2,0:T(8,128)(2,1)} %param.18) | copy-start | bytes 8650756
  192.4 2.7 copy-start.3
  217.7 5.2 %copy-start.8 = (f32[128,6]{0,1:T(8,128)S(1)}, f32[128,6]{0,1:T(8,128)}, u32[]{:S(2)}) copy-start(f32[128,6]{0,1:T(8,128)} %param.22) | copy-start | bytes 9220
  217.7 76.4 %all-to-all-start.1 = ((bf16[8,2,96,2048]{3,2,1,0:T(8,128)(2,1)}), bf16[8,2,96,2048]{3,2,1,0:T(8,128)(2,1)}, u32[]{:S(2)}, u32[]{:S(2)}) async-start(bf16[8,2,96,2048]{3,2,1,0:T(8,128)(2,1)} %copy.58), calls=%async_computation.2 | async-start | bytes 12582912 | tf_op jit(solution)/shard_map/all_to_all | solution.py:122
  222.6 115.0 %reduce-scatter.5.cloned.1.call-start = ((), (), s32[]{:S(2)}) async-start(), calls=%async_computation.7 | async-start | bytes 655360 | tf_op jit(solution)/shard_map/reduce_scatter | solution.py:137
  304.8 34.4 %copy-start.1 = (bf16[2,352,2048]{2,1,0:T(8,128)(2,1)S(1)}, bf16[2,352,2048]{2,1,0:T(8,128)(2,1)}, u32[]{:S(2)}) copy-start(bf16[2,352,2048]{2,1,0:T(8,128)(2,1)} %param.20) | copy-start | bytes 8650756
  311.5 26.0 %copy-start.5 = (bf16[32,2048]{1,0:T(8,128)(2,1)S(1)}, bf16[32,2048]{1,0:T(8,128)(2,1)}, u32[]{:S(2)}) copy-start(bf16[32,2048]{1,0:T(8,128)(2,1)} %reduce-scatter.3.cloned.1.call-done) | copy-start | bytes 393220
Sparse Core Ops, SparseCore 0:
  9.2 26.1 all-gather.2
  37.3 23.3 all-gather.4
  67.2 21.8 reduce-scatter.2
  319.1 18.3 reduce-scatter.4
where the time goes:
time: 346 us
  waiting for transfers between devices  152 us (44%)
  blocking collectives  90.7 us (26%)
  local copies, waits for them, and re-layouts  44.6 us (13%)
  matrix products  22.5 us (7%)
  other arithmetic  17.8 us (5%)
  between operations  13.3 us (4%)
  starting transfers between devices  5.21 us (2%)
    all_to_all x1, blocking collectives, per_device(): lax.all_to_all(outgoing, 'seq', split_axis=0, concat_axis=0, tiled=True)  75.3 us
    all_to_all x1, waiting for transfers between devices, per_device(): lax.all_to_all(expert_block(lax.all_to_all(outgoing, 'seq', split_axis=0,...  71.2 us
    all_gather x1, waiting for transfers between devices, per_device(): key_piece = lax.all_gather(key_rows, 'seq', axis=0, tiled=True)  22 us
    all_gather x1, waiting for transfers between devices, per_device(): value_piece = lax.all_gather(value_rows, 'seq', axis=0, tiled=True)  21.6 us
    reduce_scatter x1, waiting for transfers between devices, per_device(): lax.psum_scatter(mixture_part.astype(jnp.bfloat16), 'exp', scatter_dimens...  18.5 us
    reduce_scatter x1, waiting for transfers between devices, per_device(): lax.psum_scatter(proj_part.astype(jnp.bfloat16), 'exp', scatter_dimension...  17.6 us
    all_gather x1, blocking collectives, per_device(): normed = lax.all_gather(own_normed, 'exp', axis=0, tiled=True)  15.4 us
    dot_general x1, matrix products, expert_block(): jnp.einsum('semf,efd->semd', inner_act, down_weight, preferred_element_ty...  11.2 us
  transfers between devices with their start and end apart: 5, of which 5 were waited for; matrix products, arithmetic and copies ran while one was open for 3% of the time, Pallas kernels for 0%

commit v1 on v0

--- a/solution.py
+++ b/solution.py
@@ -6,6 +6,18 @@
 HD = 128
 TOPK = 6
 BLK = 512
+
+
+def collect(x, axis, dim):
+    ways, here = (lax.axis_size(axis), lax.axis_index(axis))
+    grown, reach = (x, 1)
+    while reach < ways:
+        theirs = lax.ppermute(grown, axis, [(d, d ^ reach) for d in range(ways)])
+        mine_first = jnp.concatenate([grown, theirs], axis=dim)
+        theirs_first = jnp.concatenate([theirs, grown], axis=dim)
+        grown = jnp.where(here & reach == 0, mine_first, theirs_first)
+        reach = 2 * reach
+    return grown
 
 
 def rms_scale(hidden, norm_gain):
@@ -56,7 +68,7 @@
     split_queries = queries.reshape(tok_rows, head_count, HD)
     score_scale = HD ** (-0.5)
     run_max = jnp.full((tok_rows, head_count), -1e30, jnp.float32)
-    key_piece = lax.all_gather(key_rows, "seq", axis=0, tiled=True)
+    key_piece = collect(key_rows, "seq", 0)
     value_piece = lax.all_gather(value_rows, "seq", axis=0, tiled=True)
     piece_rows = key_piece.shape[0]
     key_pos = jnp.arange(piece_rows, dtype=jnp.int32)

time: 346 us -> 327 us (0.945)
  waiting for transfers between devices: 152 us -> 122 us
  starting transfers between devices: 5.21 us -> 9.97 us
  other arithmetic: 17.8 us -> 21.4 us
    all_gather x1 -> x0, waiting for transfers between devices: 22 us -> none  [per_device(): key_piece = lax.all_gather(key_rows, 'seq', axis=0, tiled=True)]
    all_gather x1, waiting for transfers between devices: 21.6 us -> 0.02 us  [per_device(): value_piece = lax.all_gather(value_rows, 'seq', axis=0, tiled=True)]
    ppermute x0 -> x3, waiting for transfers between devices: none -> 13.8 us  [collect(): theirs = lax.ppermute(grown, axis, [(d, d ^ reach) for d in range(ways)])]
    ppermute x0 -> x3, starting transfers between devices: none -> 4.79 us  [collect(): theirs = lax.ppermute(grown, axis, [(d, d ^ reach) for d in range(ways)])]
  transfers between devices with their start and end apart: 5 -> 7, of which waited for: 5 -> 5; matrix products, arithmetic and copies ran while one was open for 3% -> 5% of each run, Pallas kernels for 0% -> 0%
where the time goes in v1:
time: 327 us; the launch traced here: 326 us
  waiting for transfers between devices  122 us (37%)
  blocking collectives  90.7 us (28%)
  local copies, waits for them, and re-layouts  46.8 us (14%)
  matrix products  21.9 us (7%)
  other arithmetic  21.4 us (7%)
  between operations  13.4 us (4%)
  starting transfers between devices  9.97 us (3%)
    all_to_all x1, blocking collectives, per_device(): lax.all_to_all(outgoing, 'seq', split_axis=0, concat_axis=0, tiled=True)  75.3 us
    all_to_all x1, waiting for transfers between devices, per_device(): lax.all_to_all(expert_block(lax.all_to_all(outgoing, 'seq', split_axis=0,...  71.2 us
    reduce_scatter x1, waiting for transfers between devices, per_device(): lax.psum_scatter(mixture_part.astype(jnp.bfloat16), 'exp', scatter_dimens...  18.5 us
    reduce_scatter x1, waiting for transfers between devices, per_device(): lax.psum_scatter(proj_part.astype(jnp.bfloat16), 'exp', scatter_dimension...  18.3 us
    all_gather x1, blocking collectives, per_device(): normed = lax.all_gather(own_normed, 'exp', axis=0, tiled=True)  15.4 us
    ppermute x3, waiting for transfers between devices, collect(): theirs = lax.ppermute(grown, axis, [(d, d ^ reach) for d in range(ways)])  13.8 us
    dot_general x1, matrix products, expert_block(): jnp.einsum('semf,efd->semd', inner_act, down_weight, preferred_element_ty...  11.2 us
    gather x1, local copies, waits for them, and re-layouts, per_device(): returned.reshape(slot_total, model_width)[slot_ids].astype(jnp.float32)  10.7 us
  transfers between devices with their start and end apart: 7, of which 5 were waited for; matrix products, arithmetic and copies ran while one was open for 5% of the time, Pallas kernels for 0%

profile of v1, /device:TPU:0, one launch (start us, length us, event | category | flops | bytes accessed | tf_op | source)
XLA Modules:
  0.0 326.2 jit_solution(11906393414688956472)
XLA Ops:
  6.5 0.0 all-gather.2.cloned.1.call-start
  6.5 0.5 collective-permute-start
  7.0 0.2 all-gather.2.cloned.1.call-update
  7.3 0.0 reduce-scatter.3.cloned.1.call-start
  7.3 0.8 fusion.55
  8.2 0.8 copy.79
  9.0 0.1 eq.89
  9.1 1.2 fusion.27
  10.3 0.0 collective-permute-done
  10.3 0.6 copy-done.6
  11.0 1.0 maximum_select_fusion.5
  12.0 3.0 collective-permute-start.1
  15.1 0.6 fusion.47
  15.7 1.8 copy.66
  17.4 3.2 reduce-window.6
  20.6 1.0 copy_bitcast_fusion.3
  21.6 0.4 collective-permute-done.1
  22.0 0.2 maximum_select_fusion.3
  22.3 1.3 collective-permute-start.2
  23.5 0.9 copy_bitcast_fusion.2
  24.5 0.1 maximum_select_fusion.4
  24.6 0.1 maximum_select_fusion.2
  24.7 13.4 %collective-permute-done.2 = bf16[512,512]{1,0:T(8,128)(2,1)S(1)} collective-permute-done((bf16[512,512]{1,0:T(8,128)(2,1)S(1)}, bf16[512,512]{1,0:T(8,128)(2,1)S(1)}, u32[]{:S(2)}, u32[]{:S(2)}) %collective-permute-start.2) | collective-permute-done | bytes 524320 | tf_op jit(solution)/shard_map/ppermute | solution.py:15
  38.1 0.1 copy_bitcast_fusion
  38.2 0.6 fusion.11
  38.9 1.3 copy-done.4
  40.2 0.5 fusion.22
  40.7 0.0 all-gather.2.cloned.1.call-done
  40.7 2.3 copy.76
  43.0 2.7 fusion.26
  45.7 0.0 copy-start.10
  45.8 0.0 copy-start.9
  45.8 0.0 copy-start.11
  45.8 1.3 convolution_convert_fusion
  47.1 0.0 reduce-scatter.3.cloned.1.call-update
  47.1 0.2 slice_reduce_fusion
  47.3 0.1 eq.85
  47.5 0.1 copy.78
  47.6 0.1 mul.75
  47.8 0.1 fusion.46
  47.9 3.4 %scatter_custom_fusion = s32[1536]{0:T(1024)S(1)} fusion(s32[768]{0:T(1024)S(1)} %fusion.57, s32[768]{0:T(1024)S(1)} %iota.36, s32[]{:T(128)} %constant.85.clone.1), kind=kCustom, calls=%fused_computation.89 | custom fusion | bytes 6148 | tf_op jit(solution)/shard_map/scatter | solution.py:128
  51.3 0.1 broadcast_in_dim.60
  51.4 18.3 %reduce-scatter.3.cloned.1.call-done = bf16[32,2048]{1,0:T(8,128)(2,1)} async-done(((bf16[128,2048]{1,0:T(8,128)(2,1)}), bf16[32,2048]{1,0:T(8,128)(2,1)}) %reduce-scatter.3.cloned.1.call-update) | async-done | bytes 131088 | tf_op jit(solution)/shard_map/reduce_scatter | solution.py:105
  69.7 1.1 multiply_reduce_fusion.1
  70.8 1.0 multiply_convert_fusion
  71.8 15.4 %all_gather.7 = bf16[128,2048]{1,0:T(8,128)(2,1)S(1)} all-gather(bf16[32,2048]{1,0:T(8,128)(2,1)S(1)} %multiply_convert_fusion), channel_id=1, replica_groups=mesh['seq'=8,'exp'=4] {'exp'}, dimensions={0}, use_global_device_ids=true | all-gather | bytes 655360 | tf_op jit(solution)/shard_map/all_gather | solution.py:113
  87.1 7.1 %gather_fusion = bf16[1536,2048]{1,0:T(8,128)(2,1)} fusion(bf16[128,2048]{1,0:T(8,128)(2,1)S(1)} %all_gather.7, s32[2048]{0:T(1024)S(1)} %pad_clamp_fusion), kind=kCustom, calls=%fused_computation | custom fusion | bytes 12589056 | tf_op jit(solution)/shard_map/gather | solution.py:132
  94.2 3.3 %broadcast_select_fusion = bf16[8,2,96,2048]{3,2,1,0:T(8,128)(2,1)S(1)} fusion(bf16[8,2,96,2048]{3,2,1,0:T(8,128)(2,1)} %bitcast.115, pred[8,2,96]{2,1,0:T(4,128)(4,1)S(1)} %broadcast_in_dim.60), kind=kLoop, calls=%fused_computation.5 | loop fusion | flops 3145728 | bytes 12584448 | tf_op jit(solution)/shard_map/jit(_where)/select_n | solution.py:132
  97.5 0.0 copy-start.13
  97.5 75.3 %all_to_all.10 = bf16[8,2,96,2048]{3,2,1,0:T(8,128)(2,1)S(1)} all-to-all(bf16[8,2,96,2048]{3,2,1,0:T(8,128)(2,1)S(1)} %broadcast_select_fusion), channel_id=1, replica_groups=mesh['seq'=8,'exp'=4] {'seq'}, dimensions={0} | all-to-all | bytes 12582912 | tf_op jit(solution)/shard_map/all_to_all | solution.py:136
  172.9 2.7 copy-done.2
  175.5 4.8 %fusion.2 = f32[2,8,96,352]{3,2,1,0:T(8,128)} fusion(bf16[8,2,96,2048]{3,2,1,0:T(8,128)(2,1)S(1)} %all_to_all.10, bf16[2,2048,352]{1,2,0:T(8,128)(2,1)S(1)} %copy-done.13), kind=kOutput, calls=%fused_computation.8 | convolution fusion | flops 2214592512 | bytes 11337728 | tf_op jit(solution)/shard_map/semd,edf->semf/dot_general | solution.py:29
  180.4 11.2 %convert_bitcast_fusion = bf16[8,2,96,2048]{3,2,0,1:T(8,128)(2,1)} fusion(bf16[2,352,2048]{2,1,0:T(8,128)(2,1)S(1)} %copy-done, f32[2,8,96,352]{3,2,1,0:T(8,128)} %fusion.2, bf16[2,2048,352]{1,2,0:T(8,128)(2,1)} %param.19, bf16[8,2,96,2048]{3,2,1,0:T(8,128)(2,1)} %copy-done.2), kind=kOutput, calls=%fused_computation.4 | convolution fusion | flops 4435574784 | bytes 20512768 | tf_op jit(solution)/shard_map/semf,efd->semd/dot_general | solution.py:34
  191.6 6.6 %copy.84 = bf16[8,2,96,2048]{3,2,1,0:T(8,128)(2,1)} copy(bf16[8,2,96,2048]{3,2,0,1:T(8,128)(2,1)} %convert_bitcast_fusion) | data formatting | bytes 12582912 | tf_op jit(solution)/shard_map/convert_element_type | solution.py:36
  198.2 4.9 %all-to-all-start.1 = ((bf16[8,2,96,2048]{3,2,1,0:T(8,128)(2,1)}), bf16[8,2,96,2048]{3,2,1,0:T(8,128)(2,1)}, u32[]{:S(2)}, u32[]{:S(2)}) async-start(bf16[8,2,96,2048]{3,2,1,0:T(8,128)(2,1)} %copy.84), calls=%async_computation.2 | async-start | bytes 12582912 | tf_op jit(solution)/shard_map/all_to_all | solution.py:134
  203.1 0.3 reduce-scatter.5.cloned.1.call-start
  203.3 0.1 copy.85
  203.5 71.2 %all-to-all-done.1 = bf16[8,2,96,2048]{3,2,1,0:T(8,128)(2,1)} async-done(((bf16[8,2,96,2048]{3,2,1,0:T(8,128)(2,1)}), bf16[8,2,96,2048]{3,2,1,0:T(8,128)(2,1)}, u32[]{:S(2)}, u32[]{:S(2)}) %all-to-all-start.1) | async-done | bytes 6291488 | tf_op jit(solution)/shard_map/all_to_all | solution.py:134
  274.6 10.7 %gather_fusion.1 = bf16[768,2048]{1,0:T(8,128)(2,1)} fusion(bf16[1536,2048]{1,0:T(8,128)(2,1)} %bitcast.15, s32[1024]{0:T(1024)S(1)} %pad_clamp_fusion.1), kind=kCustom, calls=%fused_computation.1 | custom fusion | bytes 6294528 | tf_op jit(solution)/shard_map/gather | solution.py:146
  285.3 6.6 %reshape.140 = f32[128,6,2048]{2,1,0:T(8,128)} reshape(bf16[768,2048]{1,0:T(8,128)(2,1)} %gather_fusion.1) | data formatting | bytes 9437184 | tf_op jit(solution)/shard_map/convert_element_type | solution.py:146
  291.9 7.6 %multiply_reduce_fusion = bf16[128,2048]{1,0:T(8,128)(2,1)} fusion(f32[128,6,2048]{2,1,0:T(8,128)} %reshape.140, f32[128,6]{1,0:T(8,128)S(1)} %copy.85), kind=kLoop, calls=%fused_computation.3 | loop fusion | flops 2883584 | bytes 6818816 | tf_op jit(solution)/shard_map/reduce_sum | solution.py:148
  299.5 0.0 reduce-scatter.5.cloned.1.call-update
  299.5 18.5 %reduce-scatter.5.cloned.1.call-done = bf16[32,2048]{1,0:T(8,128)(2,1)} async-done(((bf16[128,2048]{1,0:T(8,128)(2,1)}), bf16[32,2048]{1,0:T(8,128)(2,1)}) %reduce-scatter.5.cloned.1.call-update) | async-done | bytes 131088 | tf_op jit(solution)/shard_map/reduce_scatter | solution.py:149
  318.0 1.7 add_convert_fusion
  (36 shorter events, 0.2 us)
Async XLA Ops:
  6.5 173.8 %copy-start = (bf16[2,352,2048]{2,1,0:T(8,128)(2,1)S(1)}, bf16[2,352,2048]{2,1,0:T(8,128)(2,1)}, u32[]{:S(2)}) copy-start(bf16[2,352,2048]{2,1,0:T(8,128)(2,1)} %param.20) | copy-start | bytes 8650756
  6.5 34.2 %all-gather.2.cloned.1.call-start = ((), (), s32[]{:S(2)}) async-start(), calls=%async_computation.4 | async-start | bytes 1179648 | tf_op jit(solution)/shard_map/all_gather | solution.py:72
  6.5 3.8 %collective-permute-start = (bf16[128,512]{1,0:T(8,128)(2,1)}, bf16[128,512]{1,0:T(8,128)(2,1)S(1)}, u32[]{:S(2)}, u32[]{:S(2)}) collective-permute-start(bf16[128,512]{1,0:T(8,128)(2,1)} %param.13), channel_id=1, source_target_pairs={{0,4},{4,0},{8,12},{12,8},{16,20},{20,16},{24,28},{28,24},{1,5},{5... | collective-permute-start | bytes 393224 | tf_op jit(solution)/shard_map/ppermute | solution.py:15
  7.3 62.4 %reduce-scatter.3.cloned.1.call-start = ((), (), s32[]{:S(2)}) async-start(), calls=%async_computation.5 | async-start | bytes 655360 | tf_op jit(solution)/shard_map/reduce_scatter | solution.py:105
  10.3 0.6 copy-start.6
  12.0 10.0 %collective-permute-start.1 = (bf16[256,512]{1,0:T(8,128)(2,1)S(1)}, bf16[256,512]{1,0:T(8,128)(2,1)S(1)}, u32[]{:S(2)}, u32[]{:S(2)}) collective-permute-start(bf16[256,512]{1,0:T(8,128)(2,1)S(1)} %maximum_select_fusion.5), channel_id=1, source_target_pairs={{0,8},{4,12},{8,0},{12,4},{16,24},{20,28},{24,16},{28,20},{1,9},{5... | collective-permute-start | bytes 786440 | tf_op jit(solution)/shard_map/ppermute | solution.py:15
  20.6 17.6 %copy-start.7 = (pred[128,1024]{0,1:T(8,128)(4,1)S(1)}, pred[128,1024]{0,1:T(8,128)(4,1)}, u32[]{:S(2)}) copy-start(pred[128,1024]{0,1:T(8,128)(4,1)} %copy.66) | copy-start | bytes 393220
  20.6 17.6 %copy-start.14 = (bf16[128,512]{1,0:T(8,128)(2,1)S(1)}, bf16[128,512]{1,0:T(8,128)(2,1)}, u32[]{:S(2)}) copy-start(bf16[128,512]{1,0:T(8,128)(2,1)} %param.12) | copy-start | bytes 393220
  22.3 15.9 %collective-permute-start.2 = (bf16[512,512]{1,0:T(8,128)(2,1)S(1)}, bf16[512,512]{1,0:T(8,128)(2,1)S(1)}, u32[]{:S(2)}, u32[]{:S(2)}) collective-permute-start(bf16[512,512]{1,0:T(8,128)(2,1)S(1)} %maximum_select_fusion.3), channel_id=1, source_target_pairs={{0,16},{4,20},{8,24},{12,28},{16,0},{20,4},{24,8},{28,12},{1,17},{... | collective-permute-start | bytes 1572872 | tf_op jit(solution)/shard_map/ppermute | solution.py:15
  38.9 1.4 copy-start.4
  38.9 4.1 %copy-start.8 = (pred[128,1024]{0,1:T(8,128)(4,1)S(1)}, pred[128,1024]{0,1:T(8,128)(4,1)}, u32[]{:S(2)}) copy-start(pred[128,1024]{0,1:T(8,128)(4,1)} %copy.66) | copy-start | bytes 393220
  43.0 2.8 copy-start.3
  45.7 1.8 copy-start.10
  45.8 23.9 %copy-start.9 = (bf16[128,2048]{1,0:T(8,128)(2,1)S(1)}, bf16[128,2048]{1,0:T(8,128)(2,1)}, u32[]{:S(2)}) copy-start(bf16[128,2048]{1,0:T(8,128)(2,1)} %param.15) | copy-start | bytes 1572868
  45.8 25.0 %copy-start.11 = (f32[2048]{0:T(1024)S(1)}, f32[2048]{0:T(1024)}, u32[]{:S(2)}) copy-start(f32[2048]{0:T(1024)} %param.17) | copy-start | bytes 24580
  97.5 78.0 %copy-start.13 = (bf16[2,2048,352]{1,2,0:T(8,128)(2,1)S(1)}, bf16[2,2048,352]{1,2,0:T(8,128)(2,1)}, u32[]{:S(2)}) copy-start(bf16[2,2048,352]{1,2,0:T(8,128)(2,1)} %param.18) | copy-start | bytes 8650756
  172.9 2.7 copy-start.2
  198.2 5.2 %copy-start.12 = (f32[128,6]{0,1:T(8,128)S(1)}, f32[128,6]{0,1:T(8,128)}, u32[]{:S(2)}) copy-start(f32[128,6]{0,1:T(8,128)} %param.22) | copy-start | bytes 9220
  198.2 76.4 %all-to-all-start.1 = ((bf16[8,2,96,2048]{3,2,1,0:T(8,128)(2,1)}), bf16[8,2,96,2048]{3,2,1,0:T(8,128)(2,1)}, u32[]{:S(2)}, u32[]{:S(2)}) async-start(bf16[8,2,96,2048]{3,2,1,0:T(8,128)(2,1)} %copy.84), calls=%async_computation.2 | async-start | bytes 12582912 | tf_op jit(solution)/shard_map/all_to_all | solution.py:134
  203.1 114.9 %reduce-scatter.5.cloned.1.call-start = ((), (), s32[]{:S(2)}) async-start(), calls=%async_computation.6 | async-start | bytes 655360 | tf_op jit(solution)/shard_map/reduce_scatter | solution.py:149
  291.9 26.1 %copy-start.5 = (bf16[32,2048]{1,0:T(8,128)(2,1)S(1)}, bf16[32,2048]{1,0:T(8,128)(2,1)}, u32[]{:S(2)}) copy-start(bf16[32,2048]{1,0:T(8,128)(2,1)} %reduce-scatter.3.cloned.1.call-done) | copy-start | bytes 393220
  291.9 27.8 %copy-start.1 = (bf16[2,352,2048]{2,1,0:T(8,128)(2,1)S(1)}, bf16[2,352,2048]{2,1,0:T(8,128)(2,1)}, u32[]{:S(2)}) copy-start(bf16[2,352,2048]{2,1,0:T(8,128)(2,1)} %param.20) | copy-start | bytes 8650756
Sparse Core Ops, SparseCore 0:
  9.2 29.1 all-gather.1
  47.2 22.4 reduce-scatter.2
  299.6 18.3 reduce-scatter.4
